TPU v7x, 32 devices: a whole 2x2x4 slice. The times are simulated.
32 devices in a mesh: seq: 8 (over z, y), head: 4 (over x, core).
Axes of the slice: x: 2, y: 2, z: 4, core: 2. Of those that a mesh axis runs over, the one named last changes fastest.
Arguments:
- block_in: bfloat16 [1, 2048, 1024], P(None, 'seq'), may hold values from -6 to 6
- upstream: bfloat16 [1, 2048, 1024], P(None, 'seq'), may hold values from -6 to 6
- first_gain: float32 [1024], replicated, may hold values from 0.5 to 1.5
- project_in: bfloat16 [1024, 4, 512], P(None, 'head'), may hold values from -0.1875 to 0.1875
- filter_taps: float32 [4, 4, 512], P(None, 'head'), may hold values from -2 to 2
- squeeze: bfloat16 [1024, 16], replicated, may hold values from -0.1875 to 0.1875
- expand: bfloat16 [16, 512], P(None, 'head'), may hold values from -0.75 to 0.75
- decay_bias: float32 [512], P('head'), may hold values from 0 to 16
- gating: bfloat16 [1024, 1024], P(None, 'head'), may hold values from -0.1875 to 0.1875
- head_scale: float32 [256], replicated, may hold values from 0.5 to 1.5
- project_out: bfloat16 [1024, 1024], P('head'), may hold values from -0.375 to 0.375
- second_gain: float32 [1024], replicated, may hold values from 0.5 to 1.5
- hidden_gate: bfloat16 [1024, 2816], P(None, 'head'), may hold values from -0.1875 to 0.1875
- hidden_lift: bfloat16 [1024, 2816], P(None, 'head'), may hold values from -0.1875 to 0.1875
- hidden_drop: bfloat16 [2816, 1024], P('head'), may hold values from -0.15625 to 0.15625
Outputs:
- block_out: bfloat16 [1, 2048, 1024], P(None, 'seq')
- input_grad: float32 [1, 2048, 1024], P(None, 'seq')
- grad_first: float32 [1024], replicated
- grad_project: float32 [1024, 4, 512], P('seq', 'head')
- grad_taps: float32 [4, 4, 512], P(None, 'head')
- grad_squeeze: float32 [1024, 16], replicated
- grad_expand: float32 [16, 512], P(None, 'head')
- grad_bias: float32 [512], P('head')
- grad_gating: float32 [1024, 1024], P('seq', 'head')
- grad_scale: float32 [256], replicated
- grad_output: float32 [1024, 1024], P('head', 'seq')
- grad_second: float32 [1024], replicated
- grad_gate: float32 [1024, 2816], P('seq', 'head')
- grad_lift: float32 [1024, 2816], P('seq', 'head')
- grad_drop: float32 [2816, 1024], P('head', 'seq')
All inputs are finite; a program needn't handle non-finite values.
Results may differ from a plain program's by a relative error of at most 0.02.
Values sent between devices are 32-bit elements; how exact they have to be, the bound alone decides.
A program may use at most 128 MiB of HBM per device.

v0:
```python
import jax
import jax.numpy as jnp
from jax import lax
from jax.sharding import PartitionSpec as P

GROUP = 64


EPS = 1e-05
NORMALIZER = 16.0
HIGH = lax.Precision.HIGHEST


def shifted(x, axis, by):
    size = lax.axis_size(axis)
    pairs = [(i, i + by) for i in range(size) if 0 <= i + by < size]
    return lax.ppermute(x, axis, pairs)


def entering(value, axis, join, neutral, backward):
    count, mine = (lax.axis_size(axis), lax.axis_index(axis))
    pieces = jax.tree.map(lambda part: lax.all_gather(part, axis), value)
    if backward:
        pieces = jax.tree.map(lambda part: part[::-1], pieces)
        mine = count - 1 - mine
    total = jax.tree.map(
        lambda part, zero: jnp.full_like(part, 0) + jnp.asarray(zero, part.dtype), value, neutral
    )

    def lap(position, total):
        longer = join(total, jax.tree.map(lambda part: part[position], pieces))
        return jax.tree.map(lambda new, old: jnp.where(position < mine, new, old), longer, total)

    return lax.fori_loop(0, count - 1, lap, total)


def product(left, right):
    return jnp.dot(left, right, preferred_element_type=jnp.float32)


def against(left, right):
    return lax.dot_general(
        left, right, (((1,), (1,)), ((), ())), preferred_element_type=jnp.float32
    )


def across(left, right):
    return lax.dot_general(
        left, right, (((0,), (0,)), ((), ())), preferred_element_type=jnp.float32
    )


def rms_scale(values):
    return lax.rsqrt(jnp.mean(values * values, axis=-1, keepdims=True) + EPS)


def rms_back(values, scale, gain, incoming):
    weighted = gain * incoming
    cube = scale * scale * scale
    return scale * weighted - values * cube * jnp.mean(values * weighted, axis=-1, keepdims=True)


def silu_grad(values):
    logistic = jax.nn.sigmoid(values)
    return logistic * (1.0 + values * (1.0 - logistic))


def causal_mask(size):
    rows = lax.broadcasted_iota(jnp.int32, (size, size), 0)
    columns = lax.broadcasted_iota(jnp.int32, (size, size), 1)
    return (columns <= rows).astype(jnp.float32)


def chain(earlier, later):
    return (earlier[0] * later[0], later[0][..., None] * earlier[1] + later[1])


def grouped(array, seqs, count):
    return array.reshape((seqs, count, GROUP) + array.shape[2:])


def local_states(decays, updates, backward):

    def step(carry, item):
        decay, update = item
        return (jnp.exp(decay)[..., None] * carry + update, carry)

    init = jnp.zeros_like(updates[:, 0])
    total, states = lax.scan(
        step, init, (jnp.moveaxis(decays, 1, 0), jnp.moveaxis(updates, 1, 0)), reverse=backward
    )
    return (jnp.moveaxis(states, 0, 1), total)


def body(
    block_in,
    upstream,
    first_gain,
    project_in,
    filter_taps,
    squeeze,
    expand,
    decay_bias,
    gating,
    head_scale,
    project_out,
    second_gain,
    hidden_gate,
    hidden_lift,
    hidden_drop,
):
    seqs, tokens, width = block_in.shape
    total_rows = seqs * tokens
    key_dim = expand.shape[1]
    value_dim = gating.shape[1]
    mixed_dim = project_in.shape[2]
    lags = filter_taps.shape[0] - 1
    count = tokens // GROUP
    taps = filter_taps.reshape(lags + 1, mixed_dim)
    weight_in = project_in.reshape(width, mixed_dim)
    residual_in = block_in.reshape(total_rows, width).astype(jnp.float32)
    scale_one = rms_scale(residual_in)
    normed_one = (residual_in * scale_one * first_gain).astype(jnp.bfloat16)
    projected = product(normed_one, weight_in).reshape(seqs, tokens, mixed_dim)
    before = shifted(projected[:, tokens - lags :], "seq", 1)
    padded = jnp.concatenate([before, projected], axis=1)
    filtered = taps[0] * projected
    for lag in range(1, lags + 1):
        filtered = filtered + taps[lag] * padded[:, lags - lag : lags - lag + tokens]
    activated_low = jax.nn.silu(filtered).astype(jnp.bfloat16)
    activated = lax.optimization_barrier(activated_low).astype(jnp.float32)
    root = key_dim ** (-0.5)
    query = grouped(activated[..., :key_dim] * root, seqs, count)
    keys = grouped(activated[..., key_dim : 2 * key_dim], seqs, count)
    values = grouped(activated[..., 2 * key_dim :], seqs, count)
    squeezed = product(normed_one, squeeze).astype(jnp.bfloat16)
    logits = product(squeezed, expand) + decay_bias
    log_decay = grouped(
        (jax.nn.log_sigmoid(logits) / NORMALIZER).reshape(seqs, tokens, key_dim), seqs, count
    )
    gate_in = product(normed_one, gating)
    mask = causal_mask(GROUP)
    running = jnp.einsum("ij,snjc->snic", mask, log_decay, precision=HIGH)
    last = running[:, :, -1]
    query_in = query * jnp.exp(running)
    key_in = keys * jnp.exp(-running)
    key_end = keys * jnp.exp(last[:, :, None] - running)
    scores = jnp.einsum("snic,snjc->snij", query_in, key_in, precision=HIGH) * mask
    updates = jnp.einsum("snjc,snjd->sncd", key_end, values, precision=HIGH)
    starts_zero, state_total = local_states(last, updates, False)
    decay_sum = jnp.sum(last, axis=1)
    decay_total = jnp.exp(decay_sum)
    identity = (jnp.ones_like(decay_total), jnp.zeros_like(state_total))
    incoming = entering((decay_total, state_total), "seq", chain, identity, False)[1]
    before_group = jnp.cumsum(last, axis=1) - last
    starts = starts_zero + jnp.exp(before_group)[..., None] * incoming[:, None]
    mixed = jnp.einsum("snij,snjd->snid", scores, values, precision=HIGH)
    mixed = mixed + jnp.einsum("snic,sncd->snid", query_in, starts, precision=HIGH)
    mixed = mixed.reshape(total_rows, value_dim)
    scale_head = rms_scale(mixed)
    normed_head = mixed * scale_head * head_scale
    gated = (normed_head * jax.nn.silu(gate_in)).astype(jnp.bfloat16)
    branch = lax.psum(product(gated, project_out), "head")
    residual = residual_in + branch
    scale_two = rms_scale(residual)
    normed_two = (residual * scale_two * second_gain).astype(jnp.bfloat16)
    gate_value = product(normed_two, hidden_gate)
    lift_value = product(normed_two, hidden_lift)
    inner = (jax.nn.silu(gate_value) * lift_value).astype(jnp.bfloat16)
    feed = lax.psum(product(inner, hidden_drop), "head")
    block_out = (residual + feed).astype(jnp.bfloat16).reshape(seqs, tokens, width)
    seed = upstream.reshape(total_rows, width)
    grad_drop = across(inner, seed)
    grad_inner = against(seed, hidden_drop)
    grad_gv = (grad_inner * lift_value * silu_grad(gate_value)).astype(jnp.bfloat16)
    grad_lv = (grad_inner * jax.nn.silu(gate_value)).astype(jnp.bfloat16)
    grad_gate = across(normed_two, grad_gv)
    grad_lift = across(normed_two, grad_lv)
    feed_grads = (
        lax.psum_scatter(grad_gate, "seq", scatter_dimension=0, tiled=True),
        lax.psum_scatter(grad_lift, "seq", scatter_dimension=0, tiled=True),
        lax.psum_scatter(grad_drop, "seq", scatter_dimension=1, tiled=True),
    )
    grad_two = lax.psum(against(grad_gv, hidden_gate) + against(grad_lv, hidden_lift), "head")
    grad_second = jnp.sum(grad_two * residual * scale_two, axis=0)
    grad_resid = seed.astype(jnp.float32) + rms_back(residual, scale_two, second_gain, grad_two)
    resid_low = grad_resid.astype(jnp.bfloat16)
    grad_output = across(gated, resid_low)
    grad_gated = against(resid_low, project_out)
    grad_gatein = (grad_gated * normed_head * silu_grad(gate_in)).astype(jnp.bfloat16)
    grad_normhead = grad_gated * jax.nn.silu(gate_in)
    grad_scale = jnp.sum(grad_normhead * mixed * scale_head, axis=0)
    grad_mixed_low = rms_back(mixed, scale_head, head_scale, grad_normhead).astype(jnp.bfloat16)
    grad_mixed = lax.optimization_barrier(grad_mixed_low).astype(jnp.float32)
    outgrad = grouped(grad_mixed.reshape(seqs, tokens, value_dim), seqs, count)
    query_end = jnp.einsum("snic,snid->sncd", query_in, outgrad, precision=HIGH)
    following_zero, back_total = local_states(last, query_end, True)
    after = entering((decay_total, back_total), "seq", chain, identity, True)[1]
    after_group = decay_sum[:, None] - jnp.cumsum(last, axis=1)
    following = following_zero + jnp.exp(after_group)[..., None] * after[:, None]
    inner_group = jnp.einsum("snid,snjd->snij", outgrad, values, precision=HIGH) * mask
    grad_query = jnp.exp(running) * (
        jnp.einsum("snij,snjc->snic", inner_group, key_in, precision=HIGH)
        + jnp.einsum("snid,sncd->snic", outgrad, starts, precision=HIGH)
    )
    grad_keys = jnp.exp(-running) * jnp.einsum(
        "snij,snic->snjc", inner_group, query_in, precision=HIGH
    )
    grad_keys = grad_keys + jnp.exp(last[:, :, None] - running) * jnp.einsum(
        "snjd,sncd->snjc", values, following, precision=HIGH
    )
    grad_values = jnp.einsum("snij,snid->snjd", scores, outgrad, precision=HIGH)
    grad_values = grad_values + jnp.einsum("snjc,sncd->snjd", key_end, following, precision=HIGH)
    grad_running = (query * grad_query - keys * grad_keys).reshape(seqs, tokens, key_dim)
    state_end = decay_total[..., None] * incoming + state_total
    beyond = jnp.sum(state_end * after, axis=-1)
    upper = jnp.transpose(causal_mask(tokens))
    suffix = jnp.einsum("ij,sjc->sic", upper, grad_running, precision=HIGH)
    grad_log = suffix + beyond[:, None]
    grad_act = jnp.concatenate(
        [
            grad_query.reshape(seqs, tokens, key_dim) * root,
            grad_keys.reshape(seqs, tokens, key_dim),
            grad_values.reshape(seqs, tokens, value_dim),
        ],
        axis=-1,
    )
    grad_filtered = grad_act * silu_grad(filtered)
    later = shifted(grad_filtered[:, :lags], "seq", -1)
    padded_back = jnp.concatenate([grad_filtered, later], axis=1)
    grad_projected = taps[0] * grad_filtered
    tap_rows = [jnp.sum(grad_filtered * projected, axis=(0, 1))]
    for lag in range(1, lags + 1):
        grad_projected = grad_projected + taps[lag] * padded_back[:, lag : lag + tokens]
        tap_rows.append(
            jnp.sum(grad_filtered * padded[:, lags - lag : lags - lag + tokens], axis=(0, 1))
        )
    grad_taps = jnp.stack(tap_rows).reshape(lags + 1, 1, mixed_dim)
    grad_projected = grad_projected.reshape(total_rows, mixed_dim).astype(jnp.bfloat16)
    grad_logits = grad_log.reshape(total_rows, key_dim) * jax.nn.sigmoid(-logits) / NORMALIZER
    grad_bias = jnp.sum(grad_logits, axis=0)
    logits_low = grad_logits.astype(jnp.bfloat16)
    grad_expand = across(squeezed, logits_low)
    squeeze_low = against(logits_low, expand).astype(jnp.bfloat16)
    grad_squeeze = across(normed_one, squeeze_low)
    grad_project = across(normed_one, grad_projected).reshape(width, 1, mixed_dim)
    grad_gating = across(normed_one, grad_gatein)
    partial_value = (
        against(grad_projected, weight_in)
        + against(grad_gatein, gating)
        + against(squeeze_low, squeeze)
    )
    grad_one = lax.psum(partial_value, "head")
    grad_first = jnp.sum(grad_one * residual_in * scale_one, axis=0)
    input_grad = (grad_resid + rms_back(residual_in, scale_one, first_gain, grad_one)).reshape(
        seqs, tokens, width
    )
    mixer_grads = (
        lax.psum_scatter(grad_project, "seq", scatter_dimension=0, tiled=True),
        lax.psum_scatter(grad_gating, "seq", scatter_dimension=0, tiled=True),
        lax.psum_scatter(grad_output, "seq", scatter_dimension=1, tiled=True),
    )
    summed = tuple(mixer_grads) + tuple(feed_grads)
    small_head = lax.psum((grad_taps, grad_expand, grad_bias, grad_first, grad_second), "seq")
    shared = lax.psum((grad_scale, grad_squeeze), ("seq", "head"))
    return (
        block_out,
        input_grad,
        small_head[3],
        summed[0],
        small_head[0],
        shared[1],
        small_head[1],
        small_head[2],
        summed[1],
        shared[0],
        summed[2],
        small_head[4],
        summed[3],
        summed[4],
        summed[5],
    )


def solution(mesh):
    in_specs = (
        P(None, "seq", None),
        P(None, "seq", None),
        P(),
        P(None, "head", None),
        P(None, "head", None),
        P(),
        P(None, "head"),
        P("head"),
        P(None, "head"),
        P(),
        P("head", None),
        P(),
        P(None, "head"),
        P(None, "head"),
        P("head", None),
    )
    out_specs = (
        P(None, "seq", None),
        P(None, "seq", None),
        P(),
        P("seq", "head", None),
        P(None, "head", None),
        P(),
        P(None, "head"),
        P("head"),
        P("seq", "head"),
        P(),
        P("head", "seq"),
        P(),
        P("seq", "head"),
        P("seq", "head"),
        P("head", "seq"),
    )
    return jax.shard_map(body, mesh=mesh, in_specs=in_specs, out_specs=out_specs, check_vma=False)
```

profile of v0, /device:TPU:0, one launch (start us, length us, event | category | flops | bytes accessed | tf_op | source)
XLA Modules:
  0.0 871.2 jit_solution(14256679517528602044)
XLA Ops:
  11.2 4.9 collective-permute-start
  20.4 4.3 while.58
  26.0 21.5 %all-gather.3 = f32[8,1,128]{2,1,0:T(1,128)S(1)} all-gather(f32[1,1,128]{2,1,0:T(1,128)S(1)} %get-tuple-element.555), channel_id=2, replica_groups=mesh['seq'=8,'head'=4] {'seq'}, dimensions={0}, use_global_device_ids=true | all-gather | bytes 4608 | tf_op jit(solution)/shard_map/all_gather | solution.py:22
  49.4 18.3 %all-gather.7.cloned.1.call-done = f32[8,128,256]{2,1,0:T(8,128)} async-done(((f32[1,128,256]{2,1,0:T(8,128)}), f32[8,128,256]{2,1,0:T(8,128)}) %all-gather.7.cloned.1.call-update) | async-done | bytes 1048592 | tf_op jit(solution)/shard_map/all_gather | solution.py:22
  67.7 7.3 while.59
  80.8 35.1 %all-reduce.7.cloned.1.call-done = f32[256,1024]{1,0:T(8,128)} async-done(((f32[256,1024]{1,0:T(8,128)}), f32[256,1024]{1,0:T(8,128)}) %all-reduce.7.cloned.1.call-update) | async-done | bytes 1048592 | tf_op jit(solution)/shard_map/psum | solution.py:163
  126.5 35.6 %all-reduce.9.cloned.1.call-done = f32[256,1024]{1,0:T(8,128)} async-done(((f32[256,1024]{1,0:T(8,128)}), f32[256,1024]{1,0:T(8,128)}) %all-reduce.9.cloned.1.call-update) | async-done | bytes 1048592 | tf_op jit(solution)/shard_map/psum | solution.py:184
  170.1 9.2 %while.60 = (s32[]{:T(128)}, f32[1,128,256]{2,1,0:T(8,128)S(1)}, f32[4,1,128,256]{3,2,1,0:T(8,128)}, f32[4,1,128]{2,1,0:T(1,128)}, f32[4,1,128,256]{3,2,1,0:T(8,128)}, /*index=5*/s32[]{:T(128)}, s32[]{:T(128)}, s32[]{:T(128)}) while((s32[]{:T(128)}, f32[1,128,256]{2,1,0:T(8,128)S(1)}, f32[4,1,128,256]{3,2,1,0:T(8,128)}, ...), condition=%wide.region_15.16_spmd.clone, body=%wide.region_14.15_spmd.clone.sunk | while | flops 131076 | bytes 657016 | solution.py:89
  180.9 2.6 fusion.121
  187.3 33.6 %all-gather.9.cloned.1.call-done = f32[8,128,256]{2,1,0:T(8,128)} async-done(((f32[1,128,256]{2,1,0:T(8,128)}), f32[8,128,256]{2,1,0:T(8,128)}) %all-gather.9.cloned.1.call-update) | async-done | bytes 1048592 | tf_op jit(solution)/shard_map/all_gather | solution.py:22
  223.2 15.3 %while.61 = (s32[]{:T(128)}, f32[1,128,256]{2,1,0:T(8,128)S(1)}, s32[]{:T(128)}, f32[8,1,128]{2,1,0:T(1,128)}, f32[8,1,128,256]{3,2,1,0:T(8,128)}, /*index=5*/s32[]{:T(128)}, s32[]{:T(128)}) while((s32[]{:T(128)}, f32[1,128,256]{2,1,0:T(8,128)S(1)}, s32[]{:T(128)}, f32[8,1,128]{2,1,0:T(1,128)}, f32[8,1,128,256]{3,2,1,0:T(8,128)}, ...), condition=%wide.region_17.18_spmd.clone, body=%wide.region_16.17_spmd.clone.sunk | while | flops 131076 | bytes 394857 | solution.py:34
  259.6 3.1 fusion.124
  262.8 3.2 fusion.125
  267.0 3.2 fusion.51
  270.8 38.8 %psum.86 = f32[256]{0:T(256)} all-reduce(f32[256]{0:T(256)S(1)} %copy-done.89), channel_id=1, replica_groups=mesh['seq'=8,'head'=4] {'seq','head'}, use_global_device_ids=true, to_apply=%region_35.36 | all-reduce | flops 256 | bytes 2048 | tf_op jit(solution)/shard_map/psum | solution.py:265
  311.4 37.7 %all-reduce = (f32[1024]{0:T(1024)}, f32[4,1,512]{2,1,0:T(1,128)}, f32[16,128]{1,0:T(8,128)}, f32[128]{0:T(128)}, f32[1024]{0:T(1024)}) all-reduce(f32[1024]{0:T(1024)S(1)} %get-tuple-element.475, f32[4,1,512]{2,1,0:T(1,128)S(1)} %reshape.447, f32[16,128]{1,0:T(8,128)S(1)} %fusion.99, ...), channel_id=1, replica_groups=mesh['seq'=8,'head'=4] {'seq'}, use_global_device_ids=true, to_apply=%region_22.23 | all-reduce | flops 6272 | bytes 50176 | tf_op jit(solution)/shard_map/psum | solution.py:264
  349.1 3.4 fusion.27
  352.5 21.5 %reduce-scatter.7.cloned.1.call-done = f32[128,1,512]{2,0,1:T(8,128)} async-done(((f32[1024,1,512]{2,0,1:T(8,128)}), f32[128,1,512]{2,0,1:T(8,128)}) %reduce-scatter.7.cloned.1.call-update) | async-done | bytes 262160 | tf_op jit(solution)/shard_map/reduce_scatter | solution.py:259
  376.0 122.0 %all-reduce.11.cloned.1.call-done = f32[1024,16]{0,1:T(8,128)} async-done(((f32[1024,16]{0,1:T(8,128)}), f32[1024,16]{0,1:T(8,128)}) %all-reduce.11.cloned.1.call-update) | async-done | bytes 65552 | tf_op jit(solution)/shard_map/psum | solution.py:265
  498.0 69.9 %reduce-scatter.11.cloned.1.call-done = f32[256,128]{1,0:T(8,128)} async-done(((f32[256,1024]{1,0:T(8,128)}), f32[256,128]{1,0:T(8,128)}) %reduce-scatter.11.cloned.1.call-update) | async-done | bytes 131088 | tf_op jit(solution)/shard_map/reduce_scatter | solution.py:261
  567.9 67.2 %reduce-scatter.9.cloned.1.call-done = f32[128,256]{1,0:T(8,128)} async-done(((f32[1024,256]{1,0:T(8,128)}), f32[128,256]{1,0:T(8,128)}) %reduce-scatter.9.cloned.1.call-update) | async-done | bytes 131088 | tf_op jit(solution)/shard_map/reduce_scatter | solution.py:260
  635.2 75.6 %reduce-scatter.13.cloned.1.call-done = f32[128,704]{0,1:T(8,128)} async-done(((f32[1024,704]{0,1:T(8,128)}), f32[128,704]{0,1:T(8,128)}) %reduce-scatter.13.cloned.1.call-update) | async-done | bytes 360464 | tf_op jit(solution)/shard_map/reduce_scatter | solution.py:180
  710.8 76.2 %reduce-scatter.15.cloned.1.call-done = f32[128,704]{0,1:T(8,128)} async-done(((f32[1024,704]{0,1:T(8,128)}), f32[128,704]{0,1:T(8,128)}) %reduce-scatter.15.cloned.1.call-update) | async-done | bytes 360464 | tf_op jit(solution)/shard_map/reduce_scatter | solution.py:181
  787.0 75.9 %reduce-scatter.17.cloned.1.call-done = f32[704,128]{1,0:T(8,128)} async-done(((f32[704,1024]{1,0:T(8,128)}), f32[704,128]{1,0:T(8,128)}) %reduce-scatter.17.cloned.1.call-update) | async-done | bytes 360464 | tf_op jit(solution)/shard_map/reduce_scatter | solution.py:182
  (343 shorter events, 105.8 us)
Async XLA Ops:
  7.2 113.7 %copy-start = (bf16[704,1024]{1,0:T(8,128)(2,1)S(1)}, bf16[704,1024]{1,0:T(8,128)(2,1)}, u32[]{:S(2)}) copy-start(bf16[704,1024]{1,0:T(8,128)(2,1)} %param.37) | copy-start | bytes 4325380
  7.2 60.5 %all-gather.7.cloned.1.call-start = ((), (), s32[]{:S(2)}) async-start(), calls=%async_computation.15 | async-start | bytes 1179648 | tf_op jit(solution)/shard_map/all_gather | solution.py:22
  11.2 6.3 collective-permute-start
  18.7 49.0 %copy-start.12 = (f32[1,256,128]{2,1,0:T(8,128)}, f32[1,256,128]{2,1,0:T(8,128)S(1)}, u32[]{:S(2)}) copy-start(f32[1,256,128]{2,1,0:T(8,128)S(1)} %slice.81) | copy-start | bytes 393220
  19.1 148.3 %copy-start.24 = (f32[1,4,64,128]{3,2,1,0:T(8,128)}, f32[1,4,64,128]{3,2,1,0:T(8,128)S(1)}, u32[]{:S(2)}) copy-start(f32[1,4,64,128]{3,2,1,0:T(8,128)S(1)} %get-tuple-element.558) | copy-start | bytes 393220
  24.7 50.9 %copy-start.16 = (f32[4,1,128,256]{3,2,1,0:T(8,128)}, f32[4,1,128,256]{3,2,1,0:T(8,128)S(1)}, u32[]{:S(2)}) copy-start(f32[4,1,128,256]{3,2,1,0:T(8,128)S(1)} %get-tuple-element.335) | copy-start | bytes 1572868
  25.3 90.6 %all-reduce.7.cloned.1.call-start = ((), (), s32[]{:S(2)}) async-start(), calls=%async_computation.6 | async-start | bytes 2097152 | tf_op jit(solution)/shard_map/psum | solution.py:163
  25.4 42.3 %copy-start.47 = (f32[64,64]{1,0:T(8,128)}, f32[64,64]{1,0:T(8,128)S(1)}, u32[]{:S(2)}) copy-start(f32[64,64]{1,0:T(8,128)S(1)} %fusion.102) | copy-start | bytes 49156
  80.8 81.4 %all-reduce.9.cloned.1.call-start = ((), (), s32[]{:S(2)}) async-start(), calls=%async_computation.7 | async-start | bytes 2097152 | tf_op jit(solution)/shard_map/psum | solution.py:184
  125.2 95.7 %all-gather.9.cloned.1.call-start = ((), (), s32[]{:S(2)}) async-start(), calls=%async_computation.16 | async-start | bytes 1179648 | tf_op jit(solution)/shard_map/all_gather | solution.py:22
  180.0 129.8 %all-reduce.13.cloned.1.call-start = ((), (), s32[]{:S(2)}) async-start(), calls=%async_computation.17 | async-start | bytes 4194304 | tf_op jit(solution)/shard_map/psum | solution.py:170
  243.0 5.7 collective-permute-start.1
  251.5 122.5 %reduce-scatter.7.cloned.1.call-start = ((), (), s32[]{:S(2)}) async-start(), calls=%async_computation.8 | async-start | bytes 2359296 | tf_op jit(solution)/shard_map/reduce_scatter | solution.py:259
  253.5 244.6 %all-reduce.11.cloned.1.call-start = ((), (), s32[]{:S(2)}) async-start(), calls=%async_computation.9 | async-start | bytes 131072 | tf_op jit(solution)/shard_map/psum | solution.py:265
  254.5 313.5 %reduce-scatter.11.cloned.1.call-start = ((), (), s32[]{:S(2)}) async-start(), calls=%async_computation.11 | async-start | bytes 1179648 | tf_op jit(solution)/shard_map/reduce_scatter | solution.py:261
  257.1 378.0 %reduce-scatter.9.cloned.1.call-start = ((), (), s32[]{:S(2)}) async-start(), calls=%async_computation.10 | async-start | bytes 1179648 | tf_op jit(solution)/shard_map/reduce_scatter | solution.py:260
  259.6 451.2 %reduce-scatter.13.cloned.1.call-start = ((), (), s32[]{:S(2)}) async-start(), calls=%async_computation.12 | async-start | bytes 3244032 | tf_op jit(solution)/shard_map/reduce_scatter | solution.py:180
  262.7 524.2 %reduce-scatter.15.cloned.1.call-start = ((), (), s32[]{:S(2)}) async-start(), calls=%async_computation.13 | async-start | bytes 3244032 | tf_op jit(solution)/shard_map/reduce_scatter | solution.py:181
  266.0 596.9 %reduce-scatter.17.cloned.1.call-start = ((), (), s32[]{:S(2)}) async-start(), calls=%async_computation.14 | async-start | bytes 3244032 | tf_op jit(solution)/shard_map/reduce_scatter | solution.py:182
  270.2 39.5 %copy-start.51 = (bf16[256,128]{1,0:T(8,128)(2,1)S(1)}, bf16[256,128]{1,0:T(8,128)(2,1)}, u32[]{:S(2)}) copy-start(bf16[256,128]{1,0:T(8,128)(2,1)} %copy-done.50) | copy-start | bytes 196612
  270.2 39.5 %copy-start.80 = (bf16[256,16]{0,1:T(8,128)(2,1)S(1)}, bf16[256,16]{0,1:T(8,128)(2,1)}, u32[]{:S(2)}) copy-start(bf16[256,16]{0,1:T(8,128)(2,1)} %copy-done.79) | copy-start | bytes 24580
  270.2 41.2 %copy-start.71 = (f32[1024]{0:T(1024)S(1)}, f32[1024]{0:T(1024)}, u32[]{:S(2)}) copy-start(f32[1024]{0:T(1024)} %get-tuple-element.473) | copy-start | bytes 12292
  270.2 41.2 %copy-start.90 = (f32[128]{0:T(128)S(1)}, f32[128]{0:T(128)}, u32[]{:S(2)}) copy-start(f32[128]{0:T(128)} %get-tuple-element.566) | copy-start | bytes 1540
  270.2 78.9 %copy-start.85 = (f32[256]{0:T(256)S(1)}, f32[256]{0:T(256)}, u32[]{:S(2)}) copy-start(f32[256]{0:T(256)} %get-tuple-element.550) | copy-start | bytes 3076
  (83 other events, 491.2 us)
Sparse Core Ops, SparseCore 0:
  25.4 42.2 all-gather.6
  80.9 34.9 all-reduce.6
  125.4 36.7 all-reduce.8
  180.1 40.7 all-gather.8
  251.6 50.4 all-reduce.12
  305.5 68.4 reduce-scatter.6
  379.6 118.3 all-reduce.10
  502.0 65.8 reduce-scatter.10
  571.9 63.1 reduce-scatter.8
  639.1 71.6 reduce-scatter.12
  714.9 71.9 reduce-scatter.14
  791.0 71.8 reduce-scatter.16
where the time goes:
time: 873 us; the launch traced here: 871 us
  waiting for transfers between devices  634 us (73%)
  blocking collectives  98 us (11%)
  matrix products  47.6 us (5%)
  other arithmetic  42.4 us (5%)
  local copies, waits for them, and re-layouts  26.4 us (3%)
  between operations  15.4 us (2%)
    psum x1, waiting for transfers between devices, body(): shared = lax.psum((grad_scale, grad_squeeze), ('seq', 'head'))  122 us
    reduce_scatter x1, waiting for transfers between devices, body(): lax.psum_scatter(grad_lift, 'seq', scatter_dimension=0, tiled=True)  76.2 us
    reduce_scatter x1, waiting for transfers between devices, body(): lax.psum_scatter(grad_drop, 'seq', scatter_dimension=1, tiled=True)  75.9 us
    reduce_scatter x1, waiting for transfers between devices, body(): lax.psum_scatter(grad_gate, 'seq', scatter_dimension=0, tiled=True)  75.6 us
    reduce_scatter x1, waiting for transfers between devices, body(): lax.psum_scatter(grad_output, 'seq', scatter_dimension=1, tiled=True)  69.9 us
    reduce_scatter x1, waiting for transfers between devices, body(): lax.psum_scatter(grad_gating, 'seq', scatter_dimension=0, tiled=True)  67.2 us
    all_gather x2, waiting for transfers between devices, entering(): pieces = jax.tree.map(lambda part: lax.all_gather(part, axis), value)  51.9 us
    psum x1, blocking collectives, body(): shared = lax.psum((grad_scale, grad_squeeze), ('seq', 'head'))  38.8 us
  transfers between devices with their start and end apart: 14, of which 12 were waited for; matrix products, arithmetic and copies ran while one was open for 4% of the time, Pallas kernels for 0%

commit v1 on v0

--- a/solution.py
+++ b/solution.py
@@ -1,6 +1,10 @@
+import functools
+
 import jax
 import jax.numpy as jnp
 from jax import lax
+from jax.experimental import pallas as pl
+from jax.experimental.pallas import tpu as pltpu
 from jax.sharding import PartitionSpec as P
 
 GROUP = 64
@@ -9,6 +13,166 @@
 EPS = 1e-05
 NORMALIZER = 16.0
 HIGH = lax.Precision.HIGHEST
+
+
+MESH = pl.DeviceIdType.MESH
+PIECES = 4
+
+
+def greet(devices):
+    barrier = pltpu.get_barrier_semaphore()
+    for device in devices:
+        pl.semaphore_signal(barrier, inc=1, device_id=device, device_id_type=MESH)
+    pl.semaphore_wait(barrier, len(devices))
+
+
+def ring_kernel(size, arrays, *refs):
+    ins, outs = refs[:arrays], refs[arrays : 2 * arrays]
+    slots = refs[2 * arrays : 3 * arrays]
+    send_sem, recv_sem = refs[3 * arrays :]
+    half = size // 2
+    me = lax.axis_index("seq")
+    mine_head = lax.axis_index("head")
+    low, high = me % 2, me // 2
+    place = high + low * (2 * half - 1 - 2 * high)
+
+    def member(position):
+        position = (position + 2 * size) % size
+        side = position // half
+        return 2 * (position + side * (2 * half - 1 - 2 * position)) + side
+
+    partners = (
+        (member(place + 1), mine_head),
+        (member(place - 1), mine_head),
+    )
+    greet(partners)
+    rows = ins[0].shape[0] // size
+    part = rows // 2
+
+    def block(array, direction, position):
+        start = pl.multiple_of(member(position) * rows + direction * part, part)
+        return ins[array].at[pl.ds(start, part)]
+
+    def copy(array, direction, step, source):
+        return pltpu.make_async_remote_copy(
+            src_ref=source,
+            dst_ref=slots[array].at[direction, step],
+            send_sem=send_sem.at[array, direction, step],
+            recv_sem=recv_sem.at[array, direction, step],
+            device_id=partners[direction],
+            device_id_type=MESH,
+        )
+
+    for array in range(arrays):
+        for direction, sign in ((0, 1), (1, -1)):
+            copy(array, direction, 0, block(array, direction, place - sign)).start()
+
+    def lap(step, carry):
+        for array in range(arrays):
+            for direction, sign in ((0, 1), (1, -1)):
+                slot = slots[array].at[direction, step - 1]
+                copy(array, direction, step - 1, slot).wait_recv()
+                local = block(array, direction, place - sign * (step + 1))
+                slot[...] = slot[...] + local[...]
+                copy(array, direction, step, slot).start()
+        return carry
+
+    lax.fori_loop(1, size - 1, lap, 0)
+    for array in range(arrays):
+        for direction in range(2):
+            slot = slots[array].at[direction, size - 2]
+            copy(array, direction, size - 2, slot).wait_recv()
+            local = block(array, direction, place)
+            outs[array][pl.ds(direction * part, part)] = slot[...] + local[...]
+
+    def finish(step, carry):
+        for array in range(arrays):
+            for direction in range(2):
+                copy(array, direction, step, slots[array].at[direction, step]).wait_send()
+        return carry
+
+    lax.fori_loop(0, size - 1, finish, 0)
+
+
+def ring_scatter(*partials):
+    size = lax.axis_size("seq")
+    arrays = len(partials)
+    rows = partials[0].shape[0] // size
+    return pl.pallas_call(
+        functools.partial(ring_kernel, size, arrays),
+        out_shape=[jax.ShapeDtypeStruct((rows, x.shape[1]), jnp.float32) for x in partials],
+        in_specs=[pl.BlockSpec(memory_space=pltpu.VMEM)] * arrays,
+        out_specs=[pl.BlockSpec(memory_space=pltpu.VMEM)] * arrays,
+        scratch_shapes=[
+            pltpu.VMEM((2, size - 1, rows // 2, x.shape[1]), jnp.float32) for x in partials
+        ]
+        + [pltpu.SemaphoreType.DMA((arrays, 2, size - 1))] * 2,
+        compiler_params=pltpu.CompilerParams(
+            collective_id=0, has_side_effects=True, vmem_limit_bytes=56 * 1024 * 1024
+        ),
+    )(*partials)
+
+
+def head_kernel(in_ref, out_ref, pair, summed, other, back, send_sem, recv_sem):
+    me = lax.axis_index("head")
+    mine_seq = lax.axis_index("seq")
+    core, chip = me % 2, me // 2
+    near = (mine_seq, chip * 2 + 1 - core)
+    far = (mine_seq, (1 - chip) * 2 + core)
+    greet((near, far))
+    half = in_ref.shape[0] // 2
+    piece = half // PIECES
+    mine = pl.multiple_of(core * half, half)
+    theirs = pl.multiple_of((1 - core) * half, half)
+
+    def copy(stage, index, source, target, device):
+        return pltpu.make_async_remote_copy(
+            src_ref=source,
+            dst_ref=target.at[pl.ds(index * piece, piece)],
+            send_sem=send_sem.at[stage, index],
+            recv_sem=recv_sem.at[stage, index],
+            device_id=device,
+            device_id_type=MESH,
+        )
+
+    first, second, third = [], [], []
+    for index in range(PIECES):
+        source = in_ref.at[pl.ds(theirs + index * piece, piece)]
+        first.append(copy(0, index, source, pair, near))
+        first[-1].start()
+    for index in range(PIECES):
+        rows = pl.ds(index * piece, piece)
+        first[index].wait_recv()
+        summed[rows] = in_ref[pl.ds(mine + index * piece, piece)] + pair[rows]
+        second.append(copy(1, index, summed.at[rows], other, far))
+        second[-1].start()
+    for index in range(PIECES):
+        rows = pl.ds(index * piece, piece)
+        second[index].wait_recv()
+        total = pl.ds(mine + index * piece, piece)
+        out_ref[total] = summed[rows] + other[rows]
+        third.append(copy(2, index, out_ref.at[total], back, near))
+        third[-1].start()
+    for index in range(PIECES):
+        third[index].wait_recv()
+        out_ref[pl.ds(theirs + index * piece, piece)] = back[pl.ds(index * piece, piece)]
+    for item in first + second + third:
+        item.wait_send()
+
+
+def head_sum(value):
+    rows, columns = value.shape
+    landing = pltpu.VMEM((rows // 2, columns), jnp.float32)
+    return pl.pallas_call(
+        head_kernel,
+        out_shape=jax.ShapeDtypeStruct(value.shape, jnp.float32),
+        in_specs=[pl.BlockSpec(memory_space=pltpu.VMEM)],
+        out_specs=pl.BlockSpec(memory_space=pltpu.VMEM),
+        scratch_shapes=[landing] * 4 + [pltpu.SemaphoreType.DMA((3, PIECES))] * 2,
+        compiler_params=pltpu.CompilerParams(
+            collective_id=1, has_side_effects=True, vmem_limit_bytes=16 * 1024 * 1024
+        ),
+    )(value)
 
 
 def shifted(x, axis, by):
@@ -160,32 +324,26 @@
     scale_head = rms_scale(mixed)
     normed_head = mixed * scale_head * head_scale
     gated = (normed_head * jax.nn.silu(gate_in)).astype(jnp.bfloat16)
-    branch = lax.psum(product(gated, project_out), "head")
+    branch = head_sum(product(gated, project_out))
     residual = residual_in + branch
     scale_two = rms_scale(residual)
     normed_two = (residual * scale_two * second_gain).astype(jnp.bfloat16)
     gate_value = product(normed_two, hidden_gate)
     lift_value = product(normed_two, hidden_lift)
     inner = (jax.nn.silu(gate_value) * lift_value).astype(jnp.bfloat16)
-    feed = lax.psum(product(inner, hidden_drop), "head")
+    feed = head_sum(product(inner, hidden_drop))
     block_out = (residual + feed).astype(jnp.bfloat16).reshape(seqs, tokens, width)
     seed = upstream.reshape(total_rows, width)
-    grad_drop = across(inner, seed)
+    grad_drop = across(seed, inner)
     grad_inner = against(seed, hidden_drop)
     grad_gv = (grad_inner * lift_value * silu_grad(gate_value)).astype(jnp.bfloat16)
     grad_lv = (grad_inner * jax.nn.silu(gate_value)).astype(jnp.bfloat16)
-    grad_gate = across(normed_two, grad_gv)
-    grad_lift = across(normed_two, grad_lv)
-    feed_grads = (
-        lax.psum_scatter(grad_gate, "seq", scatter_dimension=0, tiled=True),
-        lax.psum_scatter(grad_lift, "seq", scatter_dimension=0, tiled=True),
-        lax.psum_scatter(grad_drop, "seq", scatter_dimension=1, tiled=True),
-    )
-    grad_two = lax.psum(against(grad_gv, hidden_gate) + against(grad_lv, hidden_lift), "head")
+    feed_both = across(normed_two, jnp.concatenate([grad_gv, grad_lv], axis=1))
+    grad_two = head_sum(against(grad_gv, hidden_gate) + against(grad_lv, hidden_lift))
     grad_second = jnp.sum(grad_two * residual * scale_two, axis=0)
     grad_resid = seed.astype(jnp.float32) + rms_back(residual, scale_two, second_gain, grad_two)
     resid_low = grad_resid.astype(jnp.bfloat16)
-    grad_output = across(gated, resid_low)
+    grad_output = across(resid_low, gated)
     grad_gated = against(resid_low, project_out)
     grad_gatein = (grad_gated * normed_head * silu_grad(gate_in)).astype(jnp.bfloat16)
     grad_normhead = grad_gated * jax.nn.silu(gate_in)
@@ -243,24 +401,29 @@
     grad_expand = across(squeezed, logits_low)
     squeeze_low = against(logits_low, expand).astype(jnp.bfloat16)
     grad_squeeze = across(normed_one, squeeze_low)
-    grad_project = across(normed_one, grad_projected).reshape(width, 1, mixed_dim)
-    grad_gating = across(normed_one, grad_gatein)
+    mixer_both = across(normed_one, jnp.concatenate([grad_projected, grad_gatein], axis=1))
     partial_value = (
         against(grad_projected, weight_in)
         + against(grad_gatein, gating)
         + against(squeeze_low, squeeze)
     )
-    grad_one = lax.psum(partial_value, "head")
+    grad_one = head_sum(partial_value)
     grad_first = jnp.sum(grad_one * residual_in * scale_one, axis=0)
     input_grad = (grad_resid + rms_back(residual_in, scale_one, first_gain, grad_one)).reshape(
         seqs, tokens, width
     )
-    mixer_grads = (
-        lax.psum_scatter(grad_project, "seq", scatter_dimension=0, tiled=True),
-        lax.psum_scatter(grad_gating, "seq", scatter_dimension=0, tiled=True),
-        lax.psum_scatter(grad_output, "seq", scatter_dimension=1, tiled=True),
-    )
-    summed = tuple(mixer_grads) + tuple(feed_grads)
+    feed_own, mixer_own, drop_own, output_own = ring_scatter(
+        feed_both, mixer_both, grad_drop, grad_output
+    )
+    hidden = grad_gv.shape[1]
+    summed = (
+        mixer_own[:, None, :mixed_dim],
+        mixer_own[:, mixed_dim:],
+        jnp.transpose(output_own),
+        feed_own[:, :hidden],
+        feed_own[:, hidden:],
+        jnp.transpose(drop_own),
+    )
     small_head = lax.psum((grad_taps, grad_expand, grad_bias, grad_first, grad_second), "seq")
     shared = lax.psum((grad_scale, grad_squeeze), ("seq", "head"))
     return (

time: 873 us -> 459 us (0.53)
  waiting for transfers between devices: 634 us -> 19.9 us
  Pallas kernels: 0 us -> 202 us
  local copies, waits for them, and re-layouts: 26.4 us -> 37.9 us
    reduce_scatter x6 -> x0, waiting for transfers between devices: 386 us -> none  [the longest x1 76.2 us: body(): lax.psum_scatter(grad_lift, 'seq', scatter_dimension=0, tiled=True)]
    pallas_call x0 -> x5, Pallas kernels: none -> 202 us  [the longest x1 135 us: ring_scatter(): pl.pallas_call(functools.partial(ring_kernel, size, arrays), out_shape=[j...]
    psum x1, waiting for transfers between devices: 122 us -> 0.01 us  [body(): shared = lax.psum((grad_scale, grad_squeeze), ('seq', 'head'))]
    psum x3 -> x0, waiting for transfers between devices: 70.7 us -> none  [the longest x1 35.6 us: body(): lax.psum(against(grad_gv, hidden_gate) + against(grad_lv, hidden_lift), '...]
    all_gather x2, waiting for transfers between devices: 51.9 us -> 16.1 us  [entering(): pieces = jax.tree.map(lambda part: lax.all_gather(part, axis), value)]
  transfers between devices with their start and end apart: 14 -> 5, of which waited for: 12 -> 2; matrix products, arithmetic and copies ran while one was open for 4% -> 7% of each run, Pallas kernels for 0% -> 33%
where the time goes in v1:
time: 459 us; the launch traced here: 457 us
  Pallas kernels  202 us (44%)
  blocking collectives  97.6 us (21%)
  matrix products  41.7 us (9%)
  local copies, waits for them, and re-layouts  37.9 us (8%)
  other arithmetic  36.9 us (8%)
  waiting for transfers between devices  19.9 us (4%)
  between operations  14.8 us (3%)
  starting transfers between devices  6.31 us (1%)
    pallas_call x1, Pallas kernels, ring_scatter(): pl.pallas_call(functools.partial(ring_kernel, size, arrays), out_shape=[j...  135 us
    pallas_call x4, Pallas kernels, head_sum(): pl.pallas_call(head_kernel, out_shape=jax.ShapeDtypeStruct(value.shape, j...  67 us
    psum x1, blocking collectives, body(): shared = lax.psum((grad_scale, grad_squeeze), ('seq', 'head'))  39 us
    psum x1, blocking collectives, body(): lax.psum((grad_taps, grad_expand, grad_bias, grad_first, grad_second), 's...  37 us
    all_gather x1, blocking collectives, entering(): pieces = jax.tree.map(lambda part: lax.all_gather(part, axis), value)  21.6 us
    mul x14, local copies, waits for them, and re-layouts, chain(): return (earlier[0] * later[0], later[0][..., None] * earlier[1] + later[1])  16.4 us
    all_gather x2, waiting for transfers between devices, entering(): pieces = jax.tree.map(lambda part: lax.all_gather(part, axis), value)  16.1 us
    unnamed x155, local copies, waits for them, and re-layouts  14 us
  transfers between devices with their start and end apart: 5, of which 2 were waited for; matrix products, arithmetic and copies ran while one was open for 7% of the time, Pallas kernels for 33%

profile of v1, /device:TPU:0, one launch (start us, length us, event | category | flops | bytes accessed | tf_op | source)
XLA Modules:
  0.0 457.2 jit_solution(17117274174090022605)
XLA Ops:
  9.2 1.9 fusion.35
  11.2 4.9 %collective-permute-start = (f32[1,3,512]{2,1,0:T(4,128)S(1)}, f32[1,3,512]{2,1,0:T(4,128)S(1)}, u32[]{:S(2)}, u32[]{:S(2)}) collective-permute-start(f32[1,3,512]{2,1,0:T(4,128)S(1)} %slice.91), channel_id=1, source_target_pairs={{0,4},{4,8},{8,12},{12,16},{16,20},{20,24},{24,28},{1,5},{5,9},{9,... | collective-permute-start | bytes 18440 | tf_op jit(solution)/shard_map/ppermute | solution.py:181
  21.1 6.7 %while.58 = (s32[]{:T(128)}, f32[1,128,256]{2,1,0:T(8,128)S(1)}, f32[4,1,128,256]{3,2,1,0:T(8,128)}, f32[4,1,128]{2,1,0:T(1,128)S(1)}, f32[4,1,128,256]{3,2,1,0:T(8,128)}, /*index=5*/s32[]{:T(128)}, s32[]{:T(128)}) while((s32[]{:T(128)}, f32[1,128,256]{2,1,0:T(8,128)S(1)}, f32[4,1,128,256]{3,2,1,0:T(8,128)}, ...), condition=%wide.region_2.3_spmd.clone, body=%wide.region_1.2_spmd.clone.sunk | while | flops 131075 | bytes 657004 | solution.py:253
  29.2 21.6 %all-gather.3 = f32[8,1,128]{2,1,0:T(1,128)S(1)} all-gather(f32[1,1,128]{2,1,0:T(1,128)S(1)} %get-tuple-element.565), channel_id=2, replica_groups=mesh['seq'=8,'head'=4] {'seq'}, dimensions={0}, use_global_device_ids=true | all-gather | bytes 4608 | tf_op jit(solution)/shard_map/all_gather | solution.py:186
  52.9 1.9 fusion.126
  54.8 16.1 %all-gather.7.cloned.1.call-done = f32[8,128,256]{2,1,0:T(8,128)} async-done(((f32[1,128,256]{2,1,0:T(8,128)}), f32[8,128,256]{2,1,0:T(8,128)}) %all-gather.7.cloned.1.call-update) | async-done | bytes 1048592 | tf_op jit(solution)/shard_map/all_gather | solution.py:186
  70.9 15.3 %while.59 = (s32[]{:T(128)}, f32[1,128,256]{2,1,0:T(8,128)S(1)}, s32[]{:T(128)}, f32[8,1,128]{2,1,0:T(1,128)}, f32[8,1,128,256]{3,2,1,0:T(8,128)}, /*index=5*/s32[]{:T(128)}, s32[]{:T(128)}) while((s32[]{:T(128)}, f32[1,128,256]{2,1,0:T(8,128)S(1)}, s32[]{:T(128)}, f32[8,1,128]{2,1,0:T(1,128)}, f32[8,1,128,256]{3,2,1,0:T(8,128)}, ...), condition=%wide.region_6.7_spmd.clone, body=%wide.region_5.6_spmd.clone.sunk | while | flops 131076 | bytes 394865 | solution.py:198
  86.2 2.3 multiply_reduce_fusion.7
  91.1 16.7 %shard_map.262 = f32[256,1024]{1,0:T(8,128)S(1)} custom-call(f32[256,1024]{1,0:T(8,128)S(1)} %fusion.127.in_ref), custom_call_target="tpu_custom_call" | custom-call | tf_op jit(solution)/shard_map/pallas_call | solution.py:166
  114.0 16.7 %shard_map.264 = f32[256,1024]{1,0:T(8,128)S(1)} custom-call(f32[256,1024]{1,0:T(8,128)S(1)} %convolution_add_fusion.2.in_ref), custom_call_target="tpu_custom_call" | custom-call | tf_op jit(solution)/shard_map/pallas_call | solution.py:166
  132.2 16.7 %shard_map.263 = f32[256,1024]{1,0:T(8,128)S(1)} custom-call(f32[256,1024]{1,0:T(8,128)S(1)} %fusion.130.in_ref), custom_call_target="tpu_custom_call" | custom-call | tf_op jit(solution)/shard_map/pallas_call | solution.py:166
  155.1 9.2 %while.60 = (s32[]{:T(128)}, f32[1,128,256]{2,1,0:T(8,128)S(1)}, f32[4,1,128,256]{3,2,1,0:T(8,128)}, f32[4,1,128]{2,1,0:T(1,128)}, f32[4,1,128,256]{3,2,1,0:T(8,128)}, /*index=5*/s32[]{:T(128)}, s32[]{:T(128)}, s32[]{:T(128)}) while((s32[]{:T(128)}, f32[1,128,256]{2,1,0:T(8,128)S(1)}, f32[4,1,128,256]{3,2,1,0:T(8,128)}, ...), condition=%wide.region_12.13_spmd.clone, body=%wide.region_11.12_spmd.clone.sunk | while | flops 131076 | bytes 657024 | solution.py:253
  166.9 39.0 %psum.54 = f32[256]{0:T(256)} all-reduce(f32[256]{0:T(256)} %get-tuple-element.488), channel_id=1, replica_groups=mesh['seq'=8,'head'=4] {'seq','head'}, use_global_device_ids=true, to_apply=%region_29.30 | all-reduce | flops 256 | bytes 2048 | tf_op jit(solution)/shard_map/psum | solution.py:428
  207.2 2.0 fusion.16
  209.2 2.3 fusion.15
  213.0 2.3 convolution_bitcast_fusion.refs_2_
  215.3 3.5 fusion.37.refs_0_
  218.8 2.3 reverse_bitcast_fusion
  221.1 15.4 %while.61 = (s32[]{:T(128)}, f32[1,128,256]{2,1,0:T(8,128)S(1)}, s32[]{:T(128)}, f32[8,1,128]{2,1,0:T(1,128)}, f32[8,1,128,256]{3,2,1,0:T(8,128)}, /*index=5*/s32[]{:T(128)}, s32[]{:T(128)}) while((s32[]{:T(128)}, f32[1,128,256]{2,1,0:T(8,128)S(1)}, s32[]{:T(128)}, f32[8,1,128]{2,1,0:T(1,128)}, f32[8,1,128,256]{3,2,1,0:T(8,128)}, ...), condition=%wide.region_14.15_spmd.clone, body=%wide.region_13.14_spmd.clone.sunk | while | flops 131076 | bytes 394865 | solution.py:198
  243.2 3.7 collective-permute-done.1
  248.9 2.4 fusion.63.refs_1_
  252.4 16.8 %shard_map.265 = f32[256,1024]{1,0:T(8,128)S(1)} custom-call(f32[256,1024]{1,0:T(8,128)S(1)} %convolution_add_fusion.in_ref), custom_call_target="tpu_custom_call" | custom-call | tf_op jit(solution)/shard_map/pallas_call | solution.py:166
  269.6 134.6 %shard_map.266 = (f32[128,1408]{1,0:T(8,128)}, f32[128,768]{1,0:T(8,128)}, f32[128,704]{1,0:T(8,128)}, f32[128,256]{1,0:T(8,128)}) custom-call(f32[1024,1408]{1,0:T(8,128)} %fusion.37.refs_0_, f32[1024,768]{1,0:T(8,128)} %fusion.63.refs_1_, f32[1024,704]{1,0:T(8,128)} %convolution_bitcast_fusion.refs_2_, f32[1024,256]{1,0:T(8,128)} %fusion.78.refs_3_), custom_call_target="tpu_custom_call" | custom-call | tf_op jit(solution)/shard_map/pallas_call | solution.py:101
  412.2 37.0 %all-reduce = (f32[1024]{0:T(1024)}, f32[4,1,512]{2,1,0:T(1,128)}, f32[16,128]{1,0:T(8,128)}, f32[128]{0:T(128)}, f32[1024]{0:T(1024)}) all-reduce(f32[1024]{0:T(1024)S(1)} %get-tuple-element.483, f32[4,1,512]{2,1,0:T(1,128)S(1)} %reshape.430, f32[16,128]{1,0:T(8,128)S(1)} %fusion.106, ...), channel_id=1, replica_groups=mesh['seq'=8,'head'=4] {'seq'}, use_global_device_ids=true, to_apply=%region_18.19 | all-reduce | flops 6272 | bytes 50176 | tf_op jit(solution)/shard_map/psum | solution.py:427
  (287 shorter events, 97.1 us)
Async XLA Ops:
  7.2 104.2 %copy-start = (bf16[704,1024]{1,0:T(8,128)(2,1)S(1)}, bf16[704,1024]{1,0:T(8,128)(2,1)}, u32[]{:S(2)}) copy-start(bf16[704,1024]{1,0:T(8,128)(2,1)} %param.37) | copy-start | bytes 4325380
  7.2 8.9 %copy-start.4 = (bf16[1,256,1024]{2,1,0:T(8,128)(2,1)S(1)}, bf16[1,256,1024]{2,1,0:T(8,128)(2,1)}, u32[]{:S(2)}) copy-start(bf16[1,256,1024]{2,1,0:T(8,128)(2,1)} %param.23) | copy-start | bytes 1572868
  7.2 8.9 %copy-start.46 = (f32[1024]{0:T(1024)S(1)}, f32[1024]{0:T(1024)}, u32[]{:S(2)}) copy-start(f32[1024]{0:T(1024)} %param.25) | copy-start | bytes 12292
  7.2 8.9 %copy-start.47 = (bf16[1024,16]{0,1:T(8,128)(2,1)S(1)}, bf16[1024,16]{0,1:T(8,128)(2,1)}, u32[]{:S(2)}) copy-start(bf16[1024,16]{0,1:T(8,128)(2,1)} %param.28) | copy-start | bytes 98308
  7.2 63.7 %all-gather.7.cloned.1.call-start = ((), (), s32[]{:S(2)}) async-start(), calls=%async_computation.1 | async-start | bytes 1179648 | tf_op jit(solution)/shard_map/all_gather | solution.py:186
  9.2 7.2 %copy-start.60 = (f32[256]{0:T(256)}, f32[256]{0:T(256)S(1)}, u32[]{:S(2)}) copy-start(f32[256]{0:T(256)S(1)} %get-tuple-element.561) | copy-start | bytes 3076
  9.2 7.2 %copy-start.68 = (bf16[16,128]{1,0:T(8,128)(2,1)S(1)}, bf16[16,128]{1,0:T(8,128)(2,1)}, u32[]{:S(2)}) copy-start(bf16[16,128]{1,0:T(8,128)(2,1)} %param.29) | copy-start | bytes 12292
  9.2 7.2 %copy-start.72 = (f32[128]{0:T(128)S(1)}, f32[128]{0:T(128)}, u32[]{:S(2)}) copy-start(f32[128]{0:T(128)} %param.30) | copy-start | bytes 1540
  9.2 8.1 %copy-start.66 = (f32[4,1,512]{2,1,0:T(1,128)S(1)}, f32[4,1,512]{2,1,0:T(1,128)}, u32[]{:S(2)}) copy-start(f32[4,1,512]{2,1,0:T(1,128)} %param.27) | copy-start | bytes 24580
  11.2 6.3 %collective-permute-start = (f32[1,3,512]{2,1,0:T(4,128)S(1)}, f32[1,3,512]{2,1,0:T(4,128)S(1)}, u32[]{:S(2)}, u32[]{:S(2)}) collective-permute-start(f32[1,3,512]{2,1,0:T(4,128)S(1)} %slice.91), channel_id=1, source_target_pairs={{0,4},{4,8},{8,12},{12,16},{16,20},{20,24},{24,28},{1,5},{5,9},{9,... | collective-permute-start | bytes 18440 | tf_op jit(solution)/shard_map/ppermute | solution.py:181
  18.7 33.3 %copy-start.10 = (f32[1,256,128]{2,1,0:T(8,128)}, f32[1,256,128]{2,1,0:T(8,128)S(1)}, u32[]{:S(2)}) copy-start(f32[1,256,128]{2,1,0:T(8,128)S(1)} %slice.97) | copy-start | bytes 393220
  19.0 32.9 %copy-start.18 = (f32[1,4,64,128]{3,2,1,0:T(8,128)}, f32[1,4,64,128]{3,2,1,0:T(8,128)S(1)}, u32[]{:S(2)}) copy-start(f32[1,4,64,128]{3,2,1,0:T(8,128)S(1)} %get-tuple-element.568) | copy-start | bytes 393220
  28.5 190.4 %all-gather.9.cloned.1.call-start = ((), (), s32[]{:S(2)}) async-start(), calls=%async_computation.2 | async-start | bytes 1179648 | tf_op jit(solution)/shard_map/all_gather | solution.py:186
  28.6 23.3 %copy-start.43 = (f32[64,64]{1,0:T(8,128)}, f32[64,64]{1,0:T(8,128)S(1)}, u32[]{:S(2)}) copy-start(f32[64,64]{1,0:T(8,128)S(1)} %fusion.109) | copy-start | bytes 49156
  52.9 33.3 %copy-start.13 = (f32[4,1,128,256]{3,2,1,0:T(8,128)S(1)}, f32[4,1,128,256]{3,2,1,0:T(8,128)}, u32[]{:S(2)}) copy-start(f32[4,1,128,256]{3,2,1,0:T(8,128)} %get-tuple-element.339) | copy-start | bytes 1572868
  112.7 19.0 %copy-start.27 = (bf16[256,704]{0,1:T(8,128)(2,1)}, bf16[256,704]{0,1:T(8,128)(2,1)S(1)}, u32[]{:S(2)}) copy-start(bf16[256,704]{0,1:T(8,128)(2,1)S(1)} %get-tuple-element.543) | copy-start | bytes 1081348
  165.0 44.3 %copy-start.17 = (bf16[256,256]{1,0:T(8,128)(2,1)S(1)}, bf16[256,256]{1,0:T(8,128)(2,1)}, u32[]{:S(2)}) copy-start(bf16[256,256]{1,0:T(8,128)(2,1)} %copy-done.16) | copy-start | bytes 393220
  165.0 284.2 %all-reduce.3.cloned.1.call-start = ((), (), s32[]{:S(2)}) async-start(), calls=%async_computation | async-start | bytes 131072 | tf_op jit(solution)/shard_map/psum | solution.py:428
  221.1 15.4 %copy-start.2 = (f32[1,128,256]{2,1,0:T(8,128)S(1)}, f32[1,128,256]{2,1,0:T(8,128)}, u32[]{:S(2)}) copy-start(f32[1,128,256]{2,1,0:T(8,128)} %copy-done.1) | copy-start | bytes 393220
  221.1 16.3 %copy-start.11 = (f32[1,256,128]{2,1,0:T(8,128)S(1)}, f32[1,256,128]{2,1,0:T(8,128)}, u32[]{:S(2)}) copy-start(f32[1,256,128]{2,1,0:T(8,128)} %copy-done.10) | copy-start | bytes 393220
  221.1 16.3 %copy-start.15 = (bf16[1,256,256]{2,1,0:T(8,128)(2,1)S(1)}, bf16[1,256,256]{2,1,0:T(8,128)(2,1)}, u32[]{:S(2)}) copy-start(bf16[1,256,256]{2,1,0:T(8,128)(2,1)} %copy-done.14) | copy-start | bytes 393220
  221.1 16.3 %copy-start.30 = (f32[1,256,128]{2,1,0:T(8,128)S(1)}, f32[1,256,128]{2,1,0:T(8,128)}, u32[]{:S(2)}) copy-start(f32[1,256,128]{2,1,0:T(8,128)} %copy-done.29) | copy-start | bytes 393220
  221.1 16.3 %copy-start.35 = (f32[1,4,64,128]{3,2,1,0:T(8,128)S(1)}, f32[1,4,64,128]{3,2,1,0:T(8,128)}, u32[]{:S(2)}) copy-start(f32[1,4,64,128]{3,2,1,0:T(8,128)} %fusion.15) | copy-start | bytes 393220
  240.9 6.0 %collective-permute-start.1 = (f32[1,3,512]{2,1,0:T(4,128)S(1)}, f32[1,3,512]{2,1,0:T(4,128)S(1)}, u32[]{:S(2)}, u32[]{:S(2)}) collective-permute-start(f32[1,3,512]{2,1,0:T(4,128)S(1)} %slice.100), channel_id=1, source_target_pairs={{4,0},{8,4},{12,8},{16,12},{20,16},{24,20},{28,24},{5,1},{9,5},{13... | collective-permute-start | bytes 18440 | tf_op jit(solution)/shard_map/ppermute | solution.py:181
  (55 other events, 129.3 us)
Sparse Core Ops, SparseCore 0:
  28.6 42.2 all-gather.6
  165.1 38.2 all-gather.8
  243.3 121.6 all-reduce.2
